TPU v7x, 512 devices: a whole 4x4x16 slice. The times are simulated.
512 devices in a mesh: bl: 32 (over y, x, core), dir: 16 (over z).
Axes of the slice: x: 4, y: 4, z: 16, core: 2. Of those that a mesh axis runs over, the one named last changes fastest.
Arguments:
- visibilities: float32 [8, 16, 8192], P(None, 'dir', 'bl'), may hold values from -24 to 24
- coherencies: bfloat16 [32, 8, 16, 8192], P('dir', None, None, 'bl'), may hold values from -6 to 6
- gain_offsets: float32 [32, 8, 512], P(None, None, 'bl'), may hold values from -1.5 to 1.5
- stations: int32 [2, 8192], P(None, 'bl'), may hold values from 0 to 511, as said below
- solve_order: int32 [32], replicated, may hold values from 0 to 31, each once
- counts: int32 [32], replicated, may hold values from 1 to 2
- damping: int32 [32], replicated, may hold values from 1 to 8
Outputs:
- gains: float32 [32, 8, 512], P(None, None, 'bl')
- residual: float32 [8, 16, 8192], P(None, 'dir', 'bl')
Inputs may be any that keep to these rules, and one draw needn't show every extreme that they name: Each baseline names two different stations. `solve_order`: each direction appears once.
All inputs are finite; a program needn't handle non-finite values.
Results may differ from a plain program's by a relative error of at most 0.0003.
Values may be sent and summed in bfloat16 or wider, within the bound.
A program may use at most 64 MiB of HBM per device.

v0:
```python
import jax
import jax.numpy as jnp
from jax import lax
from jax.sharding import PartitionSpec as P

LM_ITERS = 2
SOLVED = 4


def matrix_entry(mat, i, j):
    return (mat[4 * i + 2 * j], mat[4 * i + 2 * j + 1])


def matmul_two(left, right):
    pieces = []
    for i in (0, 1):
        for j in (0, 1):
            left_r0, left_i0 = matrix_entry(left, i, 0)
            left_r1, left_i1 = matrix_entry(left, i, 1)
            right_r0, right_i0 = matrix_entry(right, 0, j)
            right_r1, right_i1 = matrix_entry(right, 1, j)
            pieces.append(
                left_r0 * right_r0 - left_i0 * right_i0 + left_r1 * right_r1 - left_i1 * right_i1
            )
            pieces.append(
                left_r0 * right_i0 + left_i0 * right_r0 + left_r1 * right_i1 + left_i1 * right_r1
            )
    return jnp.stack(pieces)


def adjoint(mat):
    return jnp.stack([mat[0], -mat[1], mat[4], -mat[5], mat[2], -mat[3], mat[6], -mat[7]])


def apply_gains(gain_p, coher_now, gain_q):
    return matmul_two(matmul_two(gain_p, coher_now), adjoint(gain_q))


def gram_parts(gram):
    return jnp.stack([gram[0], gram[6], gram[2], gram[3]])


def station_terms(gain_p, gain_q, coher_now, target):
    z_rows = matmul_two(coher_now, adjoint(gain_q))
    y_rows = matmul_two(adjoint(coher_now), adjoint(gain_p))
    leading_endpoint = jnp.concatenate(
        [matmul_two(target, adjoint(z_rows)), gram_parts(matmul_two(z_rows, adjoint(z_rows)))], 0
    )
    second = jnp.concatenate(
        [
            matmul_two(adjoint(target), adjoint(y_rows)),
            gram_parts(matmul_two(y_rows, adjoint(y_rows))),
        ],
        0,
    )
    return (jnp.sum(leading_endpoint, axis=1), jnp.sum(second, axis=1))


def solve_station(gathered_sums, gain_now, damp_value):
    numerator = gathered_sums[:8] + damp_value * gain_now
    diag_a = gathered_sums[8] + damp_value
    diag_d = gathered_sums[9] + damp_value
    cross_r = gathered_sums[10]
    cross_i = gathered_sums[11]
    determinant = diag_a * diag_d - cross_r * cross_r - cross_i * cross_i
    zeros_row = jnp.zeros_like(determinant)
    inverse = (
        jnp.stack([diag_d, zeros_row, -cross_r, -cross_i, -cross_r, cross_i, diag_a, zeros_row])
        / determinant
    )
    return matmul_two(numerator, inverse)


def on_device(visibilities, coherencies, gain_offsets, stations, solve_order, counts, damping):
    identity = jnp.zeros((8,), jnp.float32).at[0].set(1.0).at[6].set(1.0)
    start = lax.all_gather(gain_offsets, "bl", axis=2, tiled=True) + identity[None, :, None]
    groups = lax.axis_size("bl")
    total_channels = coherencies.shape[2]
    station_count = start.shape[2]
    damping_factor = visibilities.shape[2] * groups * total_channels / station_count
    coher_all = lax.all_to_all(coherencies, "dir", 2, 0, tiled=True)
    ends_p = jnp.take(start, stations[0], axis=2)
    ends_q = jnp.take(start, stations[1], axis=2)
    gain_p = jnp.transpose(ends_p, (1, 0, 2))[:, :, None, :]
    gain_q = jnp.transpose(ends_q, (1, 0, 2))[:, :, None, :]
    coher_f32 = jnp.transpose(coher_all, (1, 0, 2, 3)).astype(jnp.float32)
    first_model = jnp.sum(apply_gains(gain_p, coher_f32, gain_q), axis=1)
    first_residual = visibilities - first_model

    def direction_model(gain_now, coher_now):
        gain_p = jnp.take(gain_now, stations[0], axis=1)[:, None, :]
        gain_q = jnp.take(gain_now, stations[1], axis=1)[:, None, :]
        return apply_gains(gain_p, coher_now, gain_q)

    def sweep(step_index, state):
        gain_table, residual = state
        which = solve_order[step_index]
        coher_now = lax.dynamic_index_in_dim(coher_all, which, 0, keepdims=False).astype(
            jnp.float32
        )
        damp_value = damping[which].astype(jnp.float32) * damping_factor
        gain_start = gain_table[which]
        target = residual + direction_model(gain_start, coher_now)

        def iterate(round_index, gain_now):
            gain_p = jnp.take(gain_now, stations[0], axis=1)[:, None, :]
            gain_q = jnp.take(gain_now, stations[1], axis=1)[:, None, :]
            leading_endpoint, second = station_terms(gain_p, gain_q, coher_now, target)
            local_sums = (
                jax.ops.segment_sum(leading_endpoint.T, stations[0], station_count)
                + jax.ops.segment_sum(second.T, stations[1], station_count)
            ).T
            gathered_sums = lax.psum(local_sums, ("bl", "dir"))
            return solve_station(gathered_sums, gain_now, damp_value)

        rounds = jnp.clip(counts[which], 0, LM_ITERS)
        gain_final = lax.fori_loop(0, rounds, iterate, gain_start)
        residual = target - direction_model(gain_final, coher_now)
        return (gain_table.at[which].set(gain_final), residual)

    gain_table, residual = lax.fori_loop(0, SOLVED, sweep, (start, first_residual))
    own_width = station_count // groups
    gains = lax.dynamic_slice_in_dim(gain_table, lax.axis_index("bl") * own_width, own_width, 2)
    return (gains, residual)


def solution(mesh):
    return jax.shard_map(
        on_device,
        mesh=mesh,
        in_specs=(
            P(None, "dir", "bl"),
            P("dir", None, None, "bl"),
            P(None, None, "bl"),
            P(None, "bl"),
            P(),
            P(),
            P(),
        ),
        out_specs=(P(None, None, "bl"), P(None, "dir", "bl")),
        check_vma=False,
    )
```

profile of v0, /device:TPU:1, one launch (start us, length us, event | category | flops | bytes accessed | tf_op | source)
XLA Modules:
  0.0 847.1 jit_solution(9811879134477437065)
XLA Ops:
  0.6 1.6 copy.1122
  2.2 15.7 %all-to-all-start = ((bf16[2,8,16,256]{3,1,0,2:T(8,128)(2,1)}), bf16[2,8,16,256]{3,1,0,2:T(8,128)(2,1)S(1)}, u32[]{:S(2)}, u32[]{:S(2)}) async-start(bf16[2,8,16,256]{3,1,0,2:T(8,128)(2,1)} %copy.1122), calls=%async_computation | async-start | bytes 262144 | tf_op jit(solution)/shard_map/all_to_all | solution.py:81
  18.0 0.8 fusion.135
  18.8 0.9 copy.1120
  19.7 27.2 %all_gather.3 = f32[32,8,512]{0,1,2:T(8,128)S(1)} all-gather(f32[32,8,16]{0,1,2:T(8,128)S(1)} %copy.1120), channel_id=1, replica_groups=mesh['bl'=32,'dir'=16] {'bl'}, dimensions={2}, use_global_device_ids=true | all-gather | bytes 540672 | tf_op jit(solution)/shard_map/all_gather | solution.py:76
  47.1 0.9 copy.1133
  48.0 2.0 gather_fusion.7
  50.0 1.6 copy.1124
  51.6 2.0 gather_fusion.6
  53.6 1.6 copy.1121
  57.4 788.4 %while.42 = (s32[]{:T(128)}, f32[32,8,512]{2,1,0:T(8,128)S(1)}, f32[8,1,256]{2,1,0:T(1,128)S(1)}, s32[32]{0:T(128)S(1)}, s32[32]{0:T(128)S(1)}, /*index=5*/bf16[...) while((s32[]{:T(128)}, f32[32,8,512]{2,1,0:T(8,128)S(1)}, ...), condition=%wide.region_8.12_spmd, body=%wide.region_1.11_spmd.sunk | while | flops 253464 | bytes 1958014 | solution.py:121
  64.8 109.2 %while.43 = (s32[]{:T(128)}, f32[8,512]{1,0:T(8,128)S(1)}, s32[]{:T(128)}, s32[2,256]{1,0:T(2,128)S(1)}, f32[8,1,256]{2,1,0:T(1,128)S(1)}, /*index=5*/f32[8,1,25...) while((s32[]{:T(128)}, f32[8,512]{1,0:T(8,128)S(1)}, ...), condition=%wide.region_7.10_spmd, body=%wide.region_3.9_spmd.sunk | while | flops 160768 | bytes 1263793 | solution.py:117
  67.0 1.5 scatter_custom_fusion.11
  69.0 1.5 scatter_custom_fusion.10
  70.6 103.1 %psum.9 = f32[12,512]{1,0:T(8,128)S(1)} all-reduce(f32[12,512]{1,0:T(8,128)S(1)} %add_bitcast_fusion.2), channel_id=1, replica_groups=mesh['bl'=32,'dir'=16] {'bl','dir'}, use_global_device_ids=true, to_apply=%region_6.8 | all-reduce | flops 6144 | bytes 49152 | tf_op jit(solution)/shard_map/while/body/eval_jaxpr/while/body/psum | solution.py:113
  174.1 0.7 gather_fusion.4
  174.9 0.7 gather_fusion.5
  175.9 0.8 and_reduce_fusion.2
  184.6 212.3 %while.43 = (s32[]{:T(128)}, f32[8,512]{1,0:T(8,128)S(1)}, s32[]{:T(128)}, s32[2,256]{1,0:T(2,128)S(1)}, f32[8,1,256]{2,1,0:T(1,128)S(1)}, /*index=5*/f32[8,1,25...) while((s32[]{:T(128)}, f32[8,512]{1,0:T(8,128)S(1)}, ...), condition=%wide.region_7.10_spmd, body=%wide.region_3.9_spmd.sunk | while | flops 160768 | bytes 1263793 | solution.py:117
  186.8 1.5 scatter_custom_fusion.11
  188.8 1.5 scatter_custom_fusion.10
  190.4 100.7 %psum.9 = f32[12,512]{1,0:T(8,128)S(1)} all-reduce(f32[12,512]{1,0:T(8,128)S(1)} %add_bitcast_fusion.2), channel_id=1, replica_groups=mesh['bl'=32,'dir'=16] {'bl','dir'}, use_global_device_ids=true, to_apply=%region_6.8 | all-reduce | flops 6144 | bytes 49152 | tf_op jit(solution)/shard_map/while/body/eval_jaxpr/while/body/psum | solution.py:113
  293.6 1.5 scatter_custom_fusion.11
  295.5 1.5 scatter_custom_fusion.10
  297.2 99.4 %psum.9 = f32[12,512]{1,0:T(8,128)S(1)} all-reduce(f32[12,512]{1,0:T(8,128)S(1)} %add_bitcast_fusion.2), channel_id=1, replica_groups=mesh['bl'=32,'dir'=16] {'bl','dir'}, use_global_device_ids=true, to_apply=%region_6.8 | all-reduce | flops 6144 | bytes 49152 | tf_op jit(solution)/shard_map/while/body/eval_jaxpr/while/body/psum | solution.py:113
  397.0 0.7 gather_fusion.4
  397.8 0.7 gather_fusion.5
  398.8 0.8 and_reduce_fusion.2
  407.5 212.1 %while.43 = (s32[]{:T(128)}, f32[8,512]{1,0:T(8,128)S(1)}, s32[]{:T(128)}, s32[2,256]{1,0:T(2,128)S(1)}, f32[8,1,256]{2,1,0:T(1,128)S(1)}, /*index=5*/f32[8,1,25...) while((s32[]{:T(128)}, f32[8,512]{1,0:T(8,128)S(1)}, ...), condition=%wide.region_7.10_spmd, body=%wide.region_3.9_spmd.sunk | while | flops 160768 | bytes 1263793 | solution.py:117
  409.7 1.5 scatter_custom_fusion.11
  411.7 1.5 scatter_custom_fusion.10
  413.3 100.4 %psum.9 = f32[12,512]{1,0:T(8,128)S(1)} all-reduce(f32[12,512]{1,0:T(8,128)S(1)} %add_bitcast_fusion.2), channel_id=1, replica_groups=mesh['bl'=32,'dir'=16] {'bl','dir'}, use_global_device_ids=true, to_apply=%region_6.8 | all-reduce | flops 6144 | bytes 49152 | tf_op jit(solution)/shard_map/while/body/eval_jaxpr/while/body/psum | solution.py:113
  516.2 1.5 scatter_custom_fusion.11
  518.1 1.5 scatter_custom_fusion.10
  519.7 99.6 %psum.9 = f32[12,512]{1,0:T(8,128)S(1)} all-reduce(f32[12,512]{1,0:T(8,128)S(1)} %add_bitcast_fusion.2), channel_id=1, replica_groups=mesh['bl'=32,'dir'=16] {'bl','dir'}, use_global_device_ids=true, to_apply=%region_6.8 | all-reduce | flops 6144 | bytes 49152 | tf_op jit(solution)/shard_map/while/body/eval_jaxpr/while/body/psum | solution.py:113
  619.7 0.7 gather_fusion.4
  620.5 0.7 gather_fusion.5
  621.5 0.8 and_reduce_fusion.2
  630.2 212.2 %while.43 = (s32[]{:T(128)}, f32[8,512]{1,0:T(8,128)S(1)}, s32[]{:T(128)}, s32[2,256]{1,0:T(2,128)S(1)}, f32[8,1,256]{2,1,0:T(1,128)S(1)}, /*index=5*/f32[8,1,25...) while((s32[]{:T(128)}, f32[8,512]{1,0:T(8,128)S(1)}, ...), condition=%wide.region_7.10_spmd, body=%wide.region_3.9_spmd.sunk | while | flops 160768 | bytes 1263793 | solution.py:117
  632.5 1.5 scatter_custom_fusion.11
  634.4 1.5 scatter_custom_fusion.10
  636.0 100.5 %psum.9 = f32[12,512]{1,0:T(8,128)S(1)} all-reduce(f32[12,512]{1,0:T(8,128)S(1)} %add_bitcast_fusion.2), channel_id=1, replica_groups=mesh['bl'=32,'dir'=16] {'bl','dir'}, use_global_device_ids=true, to_apply=%region_6.8 | all-reduce | flops 6144 | bytes 49152 | tf_op jit(solution)/shard_map/while/body/eval_jaxpr/while/body/psum | solution.py:113
  739.0 1.5 scatter_custom_fusion.11
  740.9 1.5 scatter_custom_fusion.10
  742.5 99.6 %psum.9 = f32[12,512]{1,0:T(8,128)S(1)} all-reduce(f32[12,512]{1,0:T(8,128)S(1)} %add_bitcast_fusion.2), channel_id=1, replica_groups=mesh['bl'=32,'dir'=16] {'bl','dir'}, use_global_device_ids=true, to_apply=%region_6.8 | all-reduce | flops 6144 | bytes 49152 | tf_op jit(solution)/shard_map/while/body/eval_jaxpr/while/body/psum | solution.py:113
  842.5 0.7 gather_fusion.4
  843.3 0.7 gather_fusion.5
  844.3 0.8 and_reduce_fusion.2
  (579 shorter events, 43.3 us)
Async XLA Ops:
  0.6 46.2 %copy-start.4 = (f32[8]{0:T(128)S(1)}, f32[8]{0:T(128)}, u32[]{:S(2)}) copy-start(f32[8]{0:T(128)} %constant.188.clone.1) | copy-start | bytes 100
  2.2 53.1 %all-to-all-start = ((bf16[2,8,16,256]{3,1,0,2:T(8,128)(2,1)}), bf16[2,8,16,256]{3,1,0,2:T(8,128)(2,1)S(1)}, u32[]{:S(2)}, u32[]{:S(2)}) async-start(bf16[2,8,16,256]{3,1,0,2:T(8,128)(2,1)} %copy.1122), calls=%async_computation | async-start | bytes 262144 | tf_op jit(solution)/shard_map/all_to_all | solution.py:81
  55.2 2.1 copy-start.3
  55.2 2.1 copy-start
  55.3 2.1 copy-start.2
  55.3 2.1 copy-start.5
  55.3 2.1 copy-start.6
  55.3 2.1 copy-start.7
  845.8 1.3 copy-start.1
where the time goes:
time: 849 us; the launch traced here: 847 us
  blocking collectives  731 us (86%)
  local copies, waits for them, and re-layouts  49.5 us (6%)
  other arithmetic  35.1 us (4%)
  starting transfers between devices  15.7 us (2%)
  loops' own time  15.3 us (2%)
    psum x7, blocking collectives, iterate(): gathered_sums = lax.psum(local_sums, ('bl', 'dir'))  703 us
    all_gather x1, blocking collectives, on_device(): lax.all_gather(gain_offsets, 'bl', axis=2, tiled=True)  27.2 us
  transfers between devices with their start and end apart: 1, of which 0 were waited for; matrix products, arithmetic and copies ran while one was open for 1% of the time, Pallas kernels for 0%

commit v1 on v0

--- a/solution.py
+++ b/solution.py
@@ -73,7 +73,15 @@
 
 def on_device(visibilities, coherencies, gain_offsets, stations, solve_order, counts, damping):
     identity = jnp.zeros((8,), jnp.float32).at[0].set(1.0).at[6].set(1.0)
-    start = lax.all_gather(gain_offsets, "bl", axis=2, tiled=True) + identity[None, :, None]
+
+    def feed_the_ladders(mesh_dim, x_in):
+        runs = []
+        for _ in range(lax.psum(1, mesh_dim)):
+            runs.append(x_in)
+        p_next = jnp.concatenate(lax.all_to_all(jnp.stack(runs), mesh_dim, 0, 0), axis=2)
+        return p_next
+
+    start = feed_the_ladders("bl", gain_offsets) + identity[None, :, None]
     groups = lax.axis_size("bl")
     total_channels = coherencies.shape[2]
     station_count = start.shape[2]

time: 849 us -> 856 us (level)
  blocking collectives: 731 us -> 700 us
  waiting for transfers between devices: 0.01 us -> 19.9 us
  starting transfers between devices: 15.7 us -> 26.5 us
    all_gather x1 -> x0, blocking collectives: 27.2 us -> none  [on_device(): lax.all_gather(gain_offsets, 'bl', axis=2, tiled=True)]
    all_to_all x0 -> x1, waiting for transfers between devices: none -> 11.5 us  [feed_the_ladders(): lax.all_to_all(jnp.stack(runs), mesh_dim, 0, 0)]
    all_to_all x0 -> x1, starting transfers between devices: none -> 10.7 us  [feed_the_ladders(): lax.all_to_all(jnp.stack(runs), mesh_dim, 0, 0)]
  transfers between devices with their start and end apart: 1 -> 2, of which waited for: 0 -> 2; matrix products, arithmetic and copies ran while one was open for 1% -> 0% of each run, Pallas kernels for 0% -> 0%
where the time goes in v1:
time: 856 us; the launch traced here: 855 us
  blocking collectives  700 us (82%)
  local copies, waits for them, and re-layouts  54 us (6%)
  other arithmetic  38.1 us (4%)
  starting transfers between devices  26.5 us (3%)
  waiting for transfers between devices  19.9 us (2%)
  loops' own time  15.6 us (2%)
    psum x7, blocking collectives, iterate(): gathered_sums = lax.psum(local_sums, ('bl', 'dir'))  700 us
  transfers between devices with their start and end apart: 2, of which 2 were waited for; matrix products, arithmetic and copies ran while one was open for 0% of the time, Pallas kernels for 0%

profile of v1, /device:TPU:1, one launch (start us, length us, event | category | flops | bytes accessed | tf_op | source)
XLA Modules:
  0.0 854.6 jit_solution(10953499605467925939)
XLA Ops:
  0.6 1.6 copy.1122
  2.2 15.7 %all-to-all-start.1 = ((bf16[2,8,16,256]{3,1,0,2:T(8,128)(2,1)}), bf16[2,8,16,256]{3,1,0,2:T(8,128)(2,1)S(1)}, u32[]{:S(2)}, u32[]{:S(2)}) async-start(bf16[2,8,16,256]{3,1,0,2:T(8,128)(2,1)} %copy.1122), calls=%async_computation.1 | async-start | bytes 262144 | tf_op jit(solution)/shard_map/all_to_all | solution.py:89
  18.0 0.8 fusion.135
  18.7 0.9 copy.1120
  19.9 1.7 reshape.1389
  21.6 8.4 all-to-all-done.1
  30.0 10.7 %all-to-all-start = ((f32[32,1,4096]{2,1,0:T(1,128)}), f32[32,1,4096]{2,1,0:T(1,128)S(1)}, u32[]{:S(2)}, u32[]{:S(2)}) async-start(f32[32,1,4096]{2,1,0:T(1,128)} %reshape.1389), calls=%async_computation | async-start | bytes 1048576 | tf_op jit(solution)/shard_map/all_to_all | solution.py:81
  40.8 11.5 %all-to-all-done = f32[32,1,4096]{2,1,0:T(1,128)S(1)} async-done(((f32[32,1,4096]{2,1,0:T(1,128)}), f32[32,1,4096]{2,1,0:T(1,128)S(1)}, u32[]{:S(2)}, u32[]{:S(2)}) %all-to-all-start) | async-done | bytes 524320 | tf_op jit(solution)/shard_map/all_to_all | solution.py:81
  52.8 1.9 reduce.16
  54.7 2.0 reshape.1390
  56.8 1.8 bitcast_add_fusion
  58.6 2.0 gather_fusion.7
  60.6 1.6 copy.1124
  62.1 2.0 gather_fusion.6
  64.2 1.6 copy.1121
  67.0 0.9 copy.1133
  68.8 784.5 %while.42 = (s32[]{:T(128)}, f32[32,8,512]{2,1,0:T(8,128)S(1)}, f32[8,1,256]{2,1,0:T(1,128)S(1)}, s32[32]{0:T(128)S(1)}, s32[32]{0:T(128)S(1)}, /*index=5*/bf16[...) while((s32[]{:T(128)}, f32[32,8,512]{2,1,0:T(8,128)S(1)}, ...), condition=%wide.region_8.12_spmd, body=%wide.region_1.11_spmd.sunk | while | flops 253464 | bytes 1958014 | solution.py:129
  76.2 106.5 %while.43 = (s32[]{:T(128)}, f32[8,512]{1,0:T(8,128)S(1)}, s32[]{:T(128)}, s32[2,256]{1,0:T(2,128)S(1)}, f32[8,1,256]{2,1,0:T(1,128)S(1)}, /*index=5*/f32[8,1,25...) while((s32[]{:T(128)}, f32[8,512]{1,0:T(8,128)S(1)}, ...), condition=%wide.region_7.10_spmd, body=%wide.region_3.9_spmd.sunk | while | flops 160768 | bytes 1263793 | solution.py:125
  78.5 1.5 scatter_custom_fusion.11
  80.4 1.5 scatter_custom_fusion.10
  82.0 100.4 %psum.9 = f32[12,512]{1,0:T(8,128)S(1)} all-reduce(f32[12,512]{1,0:T(8,128)S(1)} %add_bitcast_fusion.2), channel_id=1, replica_groups=mesh['bl'=32,'dir'=16] {'bl','dir'}, use_global_device_ids=true, to_apply=%region_6.8 | all-reduce | flops 6144 | bytes 49152 | tf_op jit(solution)/shard_map/while/body/eval_jaxpr/while/body/psum | solution.py:121
  182.9 0.7 gather_fusion.4
  183.7 0.7 gather_fusion.5
  193.3 211.4 %while.43 = (s32[]{:T(128)}, f32[8,512]{1,0:T(8,128)S(1)}, s32[]{:T(128)}, s32[2,256]{1,0:T(2,128)S(1)}, f32[8,1,256]{2,1,0:T(1,128)S(1)}, /*index=5*/f32[8,1,25...) while((s32[]{:T(128)}, f32[8,512]{1,0:T(8,128)S(1)}, ...), condition=%wide.region_7.10_spmd, body=%wide.region_3.9_spmd.sunk | while | flops 160768 | bytes 1263793 | solution.py:125
  195.5 1.5 scatter_custom_fusion.11
  197.4 1.5 scatter_custom_fusion.10
  199.1 98.9 %psum.9 = f32[12,512]{1,0:T(8,128)S(1)} all-reduce(f32[12,512]{1,0:T(8,128)S(1)} %add_bitcast_fusion.2), channel_id=1, replica_groups=mesh['bl'=32,'dir'=16] {'bl','dir'}, use_global_device_ids=true, to_apply=%region_6.8 | all-reduce | flops 6144 | bytes 49152 | tf_op jit(solution)/shard_map/while/body/eval_jaxpr/while/body/psum | solution.py:121
  300.5 1.5 scatter_custom_fusion.11
  302.4 1.5 scatter_custom_fusion.10
  304.1 100.3 %psum.9 = f32[12,512]{1,0:T(8,128)S(1)} all-reduce(f32[12,512]{1,0:T(8,128)S(1)} %add_bitcast_fusion.2), channel_id=1, replica_groups=mesh['bl'=32,'dir'=16] {'bl','dir'}, use_global_device_ids=true, to_apply=%region_6.8 | all-reduce | flops 6144 | bytes 49152 | tf_op jit(solution)/shard_map/while/body/eval_jaxpr/while/body/psum | solution.py:121
  404.8 0.7 gather_fusion.4
  405.6 0.7 gather_fusion.5
  415.2 212.1 %while.43 = (s32[]{:T(128)}, f32[8,512]{1,0:T(8,128)S(1)}, s32[]{:T(128)}, s32[2,256]{1,0:T(2,128)S(1)}, f32[8,1,256]{2,1,0:T(1,128)S(1)}, /*index=5*/f32[8,1,25...) while((s32[]{:T(128)}, f32[8,512]{1,0:T(8,128)S(1)}, ...), condition=%wide.region_7.10_spmd, body=%wide.region_3.9_spmd.sunk | while | flops 160768 | bytes 1263793 | solution.py:125
  417.5 1.5 scatter_custom_fusion.11
  419.4 1.5 scatter_custom_fusion.10
  421.0 99.5 %psum.9 = f32[12,512]{1,0:T(8,128)S(1)} all-reduce(f32[12,512]{1,0:T(8,128)S(1)} %add_bitcast_fusion.2), channel_id=1, replica_groups=mesh['bl'=32,'dir'=16] {'bl','dir'}, use_global_device_ids=true, to_apply=%region_6.8 | all-reduce | flops 6144 | bytes 49152 | tf_op jit(solution)/shard_map/while/body/eval_jaxpr/while/body/psum | solution.py:121
  523.0 1.5 scatter_custom_fusion.11
  524.9 1.5 scatter_custom_fusion.10
  526.6 100.5 %psum.9 = f32[12,512]{1,0:T(8,128)S(1)} all-reduce(f32[12,512]{1,0:T(8,128)S(1)} %add_bitcast_fusion.2), channel_id=1, replica_groups=mesh['bl'=32,'dir'=16] {'bl','dir'}, use_global_device_ids=true, to_apply=%region_6.8 | all-reduce | flops 6144 | bytes 49152 | tf_op jit(solution)/shard_map/while/body/eval_jaxpr/while/body/psum | solution.py:121
  628.2 0.7 gather_fusion.5
  637.9 212.1 %while.43 = (s32[]{:T(128)}, f32[8,512]{1,0:T(8,128)S(1)}, s32[]{:T(128)}, s32[2,256]{1,0:T(2,128)S(1)}, f32[8,1,256]{2,1,0:T(1,128)S(1)}, /*index=5*/f32[8,1,25...) while((s32[]{:T(128)}, f32[8,512]{1,0:T(8,128)S(1)}, ...), condition=%wide.region_7.10_spmd, body=%wide.region_3.9_spmd.sunk | while | flops 160768 | bytes 1263793 | solution.py:125
  640.1 1.5 scatter_custom_fusion.11
  642.0 1.5 scatter_custom_fusion.10
  643.6 99.6 %psum.9 = f32[12,512]{1,0:T(8,128)S(1)} all-reduce(f32[12,512]{1,0:T(8,128)S(1)} %add_bitcast_fusion.2), channel_id=1, replica_groups=mesh['bl'=32,'dir'=16] {'bl','dir'}, use_global_device_ids=true, to_apply=%region_6.8 | all-reduce | flops 6144 | bytes 49152 | tf_op jit(solution)/shard_map/while/body/eval_jaxpr/while/body/psum | solution.py:121
  745.7 1.5 scatter_custom_fusion.11
  747.7 1.5 scatter_custom_fusion.10
  749.3 100.5 %psum.9 = f32[12,512]{1,0:T(8,128)S(1)} all-reduce(f32[12,512]{1,0:T(8,128)S(1)} %add_bitcast_fusion.2), channel_id=1, replica_groups=mesh['bl'=32,'dir'=16] {'bl','dir'}, use_global_device_ids=true, to_apply=%region_6.8 | all-reduce | flops 6144 | bytes 49152 | tf_op jit(solution)/shard_map/while/body/eval_jaxpr/while/body/psum | solution.py:121
  850.9 0.7 gather_fusion.5
  (585 shorter events, 47.9 us)
Async XLA Ops:
  2.2 27.8 %all-to-all-start.1 = ((bf16[2,8,16,256]{3,1,0,2:T(8,128)(2,1)}), bf16[2,8,16,256]{3,1,0,2:T(8,128)(2,1)S(1)}, u32[]{:S(2)}, u32[]{:S(2)}) async-start(bf16[2,8,16,256]{3,1,0,2:T(8,128)(2,1)} %copy.1122), calls=%async_computation.1 | async-start | bytes 262144 | tf_op jit(solution)/shard_map/all_to_all | solution.py:89
  30.0 22.3 %all-to-all-start = ((f32[32,1,4096]{2,1,0:T(1,128)}), f32[32,1,4096]{2,1,0:T(1,128)S(1)}, u32[]{:S(2)}, u32[]{:S(2)}) async-start(f32[32,1,4096]{2,1,0:T(1,128)} %reshape.1389), calls=%async_computation | async-start | bytes 1048576 | tf_op jit(solution)/shard_map/all_to_all | solution.py:81
  40.7 16.0 %copy-start.4 = (f32[8]{0:T(128)S(1)}, f32[8]{0:T(128)}, u32[]{:S(2)}) copy-start(f32[8]{0:T(128)} %constant.188.clone.1) | copy-start | bytes 100
  66.9 1.8 copy-start.3
  66.9 1.8 copy-start
  67.0 1.8 copy-start.2
  67.0 1.8 copy-start.5
  67.0 1.8 copy-start.6
  67.0 1.8 copy-start.7
  853.3 1.3 copy-start.1
